TPU v7x, 256 devices: a whole 4x4x8 slice. The times are simulated.
256 devices in a mesh: rows: 4 (over y), past: 64 (over x, z, core).
Axes of the slice: x: 4, y: 4, z: 8, core: 2. Of those that a mesh axis runs over, the one named last changes fastest.
Arguments:
- tile_left: float32 [4, 64, 1024, 128], P('rows', 'past'), may hold values from -0.0625 to 0.0625
- tile_right: float32 [4, 64, 1024, 128], P('rows', 'past'), may hold values from -0.1875 to 0.1875
- diag_left: float32 [64, 1024, 128], P('past', 'rows'), may hold values from -6 to 6
- diag_right: float32 [64, 1024, 128], P('past', 'rows'), may hold values from -0.1875 to 0.1875
- present: int32 [4, 64], P('rows', 'past'), may hold values 0 or 1
- old_left: float32 [4, 1024, 128], P('rows'), may hold values from -6 to 6
- old_right: float32 [4, 1024, 128], P('rows'), may hold values from -0.1875 to 0.1875
- start: float32 [4, 1024, 128], P('rows'), may hold values from -6 to 6
Outputs:
- left: float32 [4, 1024, 128], P('rows')
- right: float32 [4, 1024, 128], P('rows')
Inputs may be any that keep to these rules, and one draw needn't show every extreme that they name: present is 1 exactly where the past tile of that tile row and panel is listed.
All inputs are finite; a program needn't handle non-finite values. No bound on the sum of `present` on one device may be relied on, other than what follows from the above.
Results may differ from a plain program's by a relative error of at most 0.00026.
Values sent between devices are 32-bit elements; how exact they have to be, the bound alone decides.
No kernel may reach another device: no remote copies, remote signals or barrier semaphores. Data moves between devices by JAX's collectives and lax.ppermute only.
A program may use at most 64 MiB of HBM per device.

v0:
```python
import math

import jax
import jax.numpy as jnp
from jax import lax
from jax.sharding import PartitionSpec as P

B = 1024
ITERS = 3


HIGH = lax.Precision.HIGHEST


def lower_inverse(gram):
    lower = jnp.linalg.cholesky(gram)
    ident = jnp.eye(gram.shape[-1], dtype=jnp.float32)
    return jax.vmap(lambda one: jax.scipy.linalg.solve_triangular(one, ident, lower=True))(lower)


def shards(tile_left, tile_right, diag_left, diag_right, present, old_left, old_right, start):
    diag_left, diag_right = (
        lax.all_gather(diag_left, "rows", axis=1, tiled=True),
        lax.all_gather(diag_right, "rows", axis=1, tiled=True),
    )
    weights = present.astype(jnp.float32)
    coupling = (
        jnp.einsum("ipbr,pbs->iprs", tile_right, diag_right, precision=HIGH)
        * weights[:, :, None, None]
    )

    def forward(block):
        inner = jnp.einsum("pbs,ibt->ipst", diag_left, block, precision=HIGH)
        middle = jnp.einsum("iprs,ipst->iprt", coupling, inner, precision=HIGH)
        summed = jnp.einsum("ipbr,iprt->ibt", tile_left, middle, precision=HIGH)
        small = jnp.einsum("ibr,ibt->irt", old_right, block, precision=HIGH)
        return (-summed, old_left, small)

    def backward(block):
        inner = jnp.einsum("ipbr,ibt->iprt", tile_left, block, precision=HIGH)
        middle = jnp.einsum("iprs,iprt->ipst", coupling, inner, precision=HIGH)
        summed = jnp.einsum("pbs,ipst->ibt", diag_left, middle, precision=HIGH)
        small = jnp.einsum("ibr,ibt->irt", old_left, block, precision=HIGH)
        return (-summed, old_right, small)

    def combine(terms, orthogonal):
        partial_value, vectors, small = terms
        total = lax.psum(partial_value, "past")
        total = total + jnp.einsum("ibr,irt->ibt", vectors, small, precision=HIGH)
        if orthogonal:
            gram = jnp.einsum("ibr,ibs->irs", total, total, precision=HIGH)
            total = jnp.einsum("ibr,isr->ibs", total, lower_inverse(gram), precision=HIGH)
        return total

    basis = combine(forward(start), True)
    for sweep in range(ITERS):
        basis = combine(forward(combine(backward(basis), True)), True)
    right = combine(backward(basis), False)
    return (basis * math.sqrt(B), right)


def solution(mesh):
    placed = (
        P("rows", "past", None, None),
        P("rows", "past", None, None),
        P("past", "rows", None),
        P("past", "rows", None),
        P("rows", "past"),
        P("rows", None, None),
        P("rows", None, None),
        P("rows", None, None),
    )
    return jax.shard_map(
        shards,
        mesh=mesh,
        in_specs=placed,
        out_specs=(P("rows", None, None), P("rows", None, None)),
        check_vma=False,
    )
```

profile of v0, /device:TPU:8, one launch (start us, length us, event | category | flops | bytes accessed | tf_op | source)
XLA Modules:
  0.0 1704.0 jit_solution(11065047977644913522)
XLA Ops:
  7.9 14.0 all_gather.7
  21.9 12.8 all_gather.6
  40.6 184.5 %all-reduce.9.cloned.1.call-done = f32[1,1024,128]{1,2,0:T(8,128)} async-done(((f32[1,1024,128]{1,2,0:T(8,128)}), f32[1,1024,128]{1,2,0:T(8,128)}) %all-reduce.9.cloned.1.call-update) | async-done | bytes 524304 | tf_op jit(solution)/shard_map/psum | solution.py:48
  225.1 1.7 fusion.9
  227.5 11.7 custom-call.18
  240.5 9.8 custom-call.19
  255.6 179.3 %all-reduce.11.cloned.1.call-done = f32[1,1024,128]{1,2,0:T(8,128)} async-done(((f32[1,1024,128]{1,2,0:T(8,128)}), f32[1,1024,128]{1,2,0:T(8,128)}) %all-reduce.11.cloned.1.call-update) | async-done | bytes 524304 | tf_op jit(solution)/shard_map/psum | solution.py:48
  435.0 1.6 fusion.11
  437.3 11.7 custom-call.20
  450.4 9.8 custom-call.21
  465.7 179.1 %all-reduce.13.cloned.1.call-done = f32[1,1024,128]{1,2,0:T(8,128)} async-done(((f32[1,1024,128]{1,2,0:T(8,128)}), f32[1,1024,128]{1,2,0:T(8,128)}) %all-reduce.13.cloned.1.call-update) | async-done | bytes 524304 | tf_op jit(solution)/shard_map/psum | solution.py:48
  644.8 1.6 fusion.13
  647.2 11.7 custom-call.22
  660.2 9.8 custom-call.23
  675.3 179.4 %all-reduce.15.cloned.1.call-done = f32[1,1024,128]{1,2,0:T(8,128)} async-done(((f32[1,1024,128]{1,2,0:T(8,128)}), f32[1,1024,128]{1,2,0:T(8,128)}) %all-reduce.15.cloned.1.call-update) | async-done | bytes 524304 | tf_op jit(solution)/shard_map/psum | solution.py:48
  854.8 1.6 fusion.15
  857.1 11.7 custom-call.24
  870.1 9.8 custom-call.25
  885.3 179.3 %all-reduce.17.cloned.1.call-done = f32[1,1024,128]{1,2,0:T(8,128)} async-done(((f32[1,1024,128]{1,2,0:T(8,128)}), f32[1,1024,128]{1,2,0:T(8,128)}) %all-reduce.17.cloned.1.call-update) | async-done | bytes 524304 | tf_op jit(solution)/shard_map/psum | solution.py:48
  1064.6 1.6 fusion.17
  1067.0 11.7 custom-call.26
  1080.0 9.8 custom-call.27
  1095.3 179.1 %all-reduce.19.cloned.1.call-done = f32[1,1024,128]{1,2,0:T(8,128)} async-done(((f32[1,1024,128]{1,2,0:T(8,128)}), f32[1,1024,128]{1,2,0:T(8,128)}) %all-reduce.19.cloned.1.call-update) | async-done | bytes 524304 | tf_op jit(solution)/shard_map/psum | solution.py:48
  1274.5 1.6 fusion.19
  1276.8 11.7 custom-call.28
  1289.9 9.8 custom-call.29
  1305.0 179.4 %all-reduce.21.cloned.1.call-done = f32[1,1024,128]{1,2,0:T(8,128)} async-done(((f32[1,1024,128]{1,2,0:T(8,128)}), f32[1,1024,128]{1,2,0:T(8,128)}) %all-reduce.21.cloned.1.call-update) | async-done | bytes 524304 | tf_op jit(solution)/shard_map/psum | solution.py:48
  1484.4 1.6 fusion.21
  1486.7 11.7 custom-call.30
  1499.8 9.8 custom-call.31
  1515.5 178.8 %all-reduce.23.cloned.1.call-done = f32[1,1024,128]{1,2,0:T(8,128)} async-done(((f32[1,1024,128]{1,2,0:T(8,128)}), f32[1,1024,128]{1,2,0:T(8,128)}) %all-reduce.23.cloned.1.call-update) | async-done | bytes 524304 | tf_op jit(solution)/shard_map/psum | solution.py:48
  1694.3 1.6 fusion.22
  (119 shorter events, 58.7 us)
Async XLA Ops:
  7.2 29.9 %copy-start = (f32[1,1,1024,128]{3,2,1,0:T(8,128)S(1)}, f32[1,1,1024,128]{3,2,1,0:T(8,128)}, u32[]{:S(2)}) copy-start(f32[1,1,1024,128]{3,2,1,0:T(8,128)} %param.11) | copy-start | bytes 1572868
  7.2 217.9 %all-reduce.9.cloned.1.call-start = ((), (), s32[]{:S(2)}) async-start(), calls=%async_computation | async-start | bytes 1048576 | tf_op jit(solution)/shard_map/psum | solution.py:48
  7.9 14.0 copy-start.5
  7.9 26.8 %copy-start.3 = (f32[1,1024,128]{2,1,0:T(8,128)S(1)}, f32[1,1024,128]{2,1,0:T(8,128)}, u32[]{:S(2)}) copy-start(f32[1,1024,128]{2,1,0:T(8,128)} %param.18) | copy-start | bytes 1572868
  34.7 1.0 copy-start.4
  38.5 1.0 copy-start.2
  38.5 186.5 %copy-start.1 = (f32[1,1024,128]{2,1,0:T(8,128)S(1)}, f32[1,1024,128]{2,1,0:T(8,128)}, u32[]{:S(2)}) copy-start(f32[1,1024,128]{2,1,0:T(8,128)} %param.16) | copy-start | bytes 1572868
  38.6 396.4 %all-reduce.11.cloned.1.call-start = ((), (), s32[]{:S(2)}) async-start(), calls=%async_computation.1 | async-start | bytes 1048576 | tf_op jit(solution)/shard_map/psum | solution.py:48
  254.4 390.4 %all-reduce.13.cloned.1.call-start = ((), (), s32[]{:S(2)}) async-start(), calls=%async_computation.2 | async-start | bytes 1048576 | tf_op jit(solution)/shard_map/psum | solution.py:48
  464.2 390.5 %all-reduce.15.cloned.1.call-start = ((), (), s32[]{:S(2)}) async-start(), calls=%async_computation.3 | async-start | bytes 1048576 | tf_op jit(solution)/shard_map/psum | solution.py:48
  674.1 390.6 %all-reduce.17.cloned.1.call-start = ((), (), s32[]{:S(2)}) async-start(), calls=%async_computation.4 | async-start | bytes 1048576 | tf_op jit(solution)/shard_map/psum | solution.py:48
  884.0 390.5 %all-reduce.19.cloned.1.call-start = ((), (), s32[]{:S(2)}) async-start(), calls=%async_computation.5 | async-start | bytes 1048576 | tf_op jit(solution)/shard_map/psum | solution.py:48
  1093.9 390.5 %all-reduce.21.cloned.1.call-start = ((), (), s32[]{:S(2)}) async-start(), calls=%async_computation.6 | async-start | bytes 1048576 | tf_op jit(solution)/shard_map/psum | solution.py:48
  1303.8 390.5 %all-reduce.23.cloned.1.call-start = ((), (), s32[]{:S(2)}) async-start(), calls=%async_computation.7 | async-start | bytes 1048576 | tf_op jit(solution)/shard_map/psum | solution.py:48
Sparse Core Ops, SparseCore 0:
  38.7 186.3 all-reduce.8
  254.5 180.4 all-reduce.10
  464.4 180.4 all-reduce.12
  674.2 180.4 all-reduce.14
  884.1 180.4 all-reduce.16
  1094.0 180.4 all-reduce.18
  1303.9 180.4 all-reduce.20
  1513.8 180.4 all-reduce.22
where the time goes:
time: 1710 us; the launch traced here: 1700 us
  waiting for transfers between devices  1440 us (84%)
  other arithmetic  161 us (9%)
  matrix products  56.9 us (3%)
  blocking collectives  26.8 us (2%)
    psum x8, waiting for transfers between devices, combine(): total = lax.psum(partial_value, 'past')  1440 us
    another operation x21, other arithmetic, lower_inverse(): lower = jnp.linalg.cholesky(gram)  86.7 us
    another operation x14, other arithmetic, lower_inverse(): jax.scipy.linalg.solve_triangular(one, ident, lower=True)  73.3 us
  transfers between devices with their start and end apart: 8, of which 8 were waited for; matrix products, arithmetic and copies ran while one was open for 1% of the time, Pallas kernels for 0%

commit v1 on v0

v1 whole, which is shorter than its diff:
```python
import math

import jax
import jax.numpy as jnp
from jax import lax
from jax.experimental import pallas as pl
from jax.experimental.pallas import tpu as pltpu
from jax.sharding import PartitionSpec as P

B = 1024
R = 128
ITERS = 3
NB = 8

HIGH = lax.Precision.HIGHEST
NN = (((1,), (0,)), ((), ()))
NT = (((1,), (1,)), ((), ()))


def lane(block, k):
    return jnp.broadcast_to(block[:, k : k + 1], block.shape)


def row(block, j):
    return jnp.broadcast_to(block[j : j + 1, :], block.shape)


def lower_inverse(gram):
    blocks = R // NB
    sub = lax.broadcasted_iota(jnp.int32, (NB, R), 0)
    col = lax.broadcasted_iota(jnp.int32, (NB, R), 1)
    schur = [gram[NB * i : NB * i + NB, :] for i in range(blocks)]
    aug = [jnp.where(col == sub + NB * i, 1.0, 0.0) for i in range(blocks)]
    out = []
    for kb in range(blocks):
        top, left = schur[kb], aug[kb]
        diag = [lane(top, NB * kb + j) for j in range(NB)]
        below = {i: [lane(schur[i], NB * kb + j) for j in range(NB)] for i in range(kb + 1, blocks)}
        pivots = jnp.ones((NB, R), jnp.float32)
        for j in range(NB):
            pivot = row(diag[j], j)
            inv = 1.0 / pivot
            pivots = jnp.where(sub == j, pivot, pivots)
            mult = jnp.where(sub > j, diag[j] * inv, 0.0)
            ups = [row(diag[jj], j) for jj in range(j + 1, NB)]
            for a, jj in enumerate(range(j + 1, NB)):
                diag[jj] = diag[jj] - mult * ups[a]
            trow, lrow = row(top, j), row(left, j)
            top = top - mult * trow
            left = left - mult * lrow
            for i in range(kb + 1, blocks):
                m = below[i][j] * inv
                for a, jj in enumerate(range(j + 1, NB)):
                    below[i][jj] = below[i][jj] - m * ups[a]
                schur[i] = schur[i] - m * trow
                aug[i] = aug[i] - m * lrow
        out.append(left * lax.rsqrt(pivots))
    return jnp.concatenate(out, axis=0)


def split(x):
    hi = x.astype(jnp.bfloat16)
    rest = x - hi.astype(jnp.float32)
    mid = rest.astype(jnp.bfloat16)
    low = (rest - mid.astype(jnp.float32)).astype(jnp.bfloat16)
    return hi, mid, low


def iterate_kernel(w_ref, start_ref, left_ref, right_ref, wh, wm, wl, yt):
    for r in range(0, B, 128):
        hi, mid, low = split(w_ref[r : r + 128, :])
        wh[r : r + 128, :] = hi
        wm[r : r + 128, :] = mid
        wl[r : r + 128, :] = low

    def mul(a, b, dims):
        return lax.dot_general(a, b, dims, preferred_element_type=jnp.float32)

    def times(block, dims):
        hi, mid, low = split(block)
        three = jnp.concatenate([hi, mid, low], axis=0)
        by_h = mul(three, wh[...], dims)
        by_m = mul(three[: 2 * R], wm[...], dims)
        by_l = mul(hi, wl[...], dims)
        return (by_h[:R] + by_h[R : 2 * R] + by_m[:R]) + (by_h[2 * R :] + by_m[R:] + by_l)

    def half(dims):
        block = yt[...]
        gram = lax.dot_general(block, block, NT, precision=HIGH, preferred_element_type=jnp.float32)
        product = times(block, dims)
        return lower_inverse(gram), block, product

    def apply(inv, block):
        return lax.dot_general(inv, block, NN, precision=HIGH, preferred_element_type=jnp.float32)

    yt[...] = times(start_ref[...].T, NT)

    def sweep(_, carry):
        inv, _, product = half(NN)
        yt[...] = apply(inv, product)
        inv, _, product = half(NT)
        yt[...] = apply(inv, product)
        return carry

    lax.fori_loop(0, ITERS, sweep, 0)
    inv, block, product = half(NN)
    left_ref[...] = (apply(inv, block) * math.sqrt(B)).T
    right_ref[...] = apply(inv, product).T


def iterate(w, start):
    shape = jax.ShapeDtypeStruct((B, R), jnp.float32)
    return pl.pallas_call(
        iterate_kernel,
        out_shape=(shape, shape),
        scratch_shapes=[
            pltpu.VMEM((B, B), jnp.bfloat16),
            pltpu.VMEM((B, B), jnp.bfloat16),
            pltpu.VMEM((B, B), jnp.bfloat16),
            pltpu.VMEM((R, B), jnp.float32),
        ],
        compiler_params=pltpu.CompilerParams(vmem_limit_bytes=56 * 1024 * 1024),
        name="iterate",
    )(w, start)


def shards(tile_left, tile_right, diag_left, diag_right, present, old_left, old_right, start):
    diag_left = lax.all_gather(diag_left[0], "rows", axis=0, tiled=True)
    diag_right = lax.all_gather(diag_right[0], "rows", axis=0, tiled=True)
    weight = present.astype(jnp.float32)[0, 0]
    coupling = jnp.einsum("br,bs->rs", tile_right[0, 0], diag_right, precision=HIGH) * weight
    scaled = -jnp.einsum("br,rs->bs", tile_left[0, 0], coupling, precision=HIGH)
    first = jnp.where(lax.axis_index("past") == 0, 1.0, 0.0)
    lhs = jnp.concatenate([scaled, old_left[0] * first], axis=1)
    rhs = jnp.concatenate([diag_left, old_right[0]], axis=1)
    partial_w = jnp.einsum("bk,ck->bc", lhs, rhs, precision=HIGH)
    w = lax.psum(partial_w, "past")
    left, right = iterate(w, start[0])
    return left[None], right[None]


def solution(mesh):
    placed = (
        P("rows", "past", None, None),
        P("rows", "past", None, None),
        P("past", "rows", None),
        P("past", "rows", None),
        P("rows", "past"),
        P("rows", None, None),
        P("rows", None, None),
        P("rows", None, None),
    )
    return jax.shard_map(
        shards,
        mesh=mesh,
        in_specs=placed,
        out_specs=(P("rows", None, None), P("rows", None, None)),
        check_vma=False,
    )
```

time: 1710 us -> 299 us (0.17)
  waiting for transfers between devices: 1440 us -> 199 us
  other arithmetic: 161 us -> 1.08 us
  matrix products: 56.9 us -> 7.72 us
  Pallas kernels: 0 us -> 48.5 us
    psum x8 -> x1, waiting for transfers between devices: 1440 us -> 199 us  [shards(): w = lax.psum(partial_w, 'past')]
    another operation x35 -> x0, other arithmetic: 160 us -> none  [the longest x21 86.7 us: lower_inverse(): lower = jnp.linalg.cholesky(gram)]
    pallas_call x0 -> x1, Pallas kernels: none -> 48.5 us  [iterate(): pl.pallas_call(iterate_kernel, out_shape=(shape, shape), scratch_shapes=[...]
    dot_general x55 -> x3, matrix products: 54.9 us -> 7.72 us  [the longest x1 5.1 us: shards(): partial_w = jnp.einsum('bk,ck->bc', lhs, rhs, precision=HIGH)]
  transfers between devices with their start and end apart: 8 -> 1, of which waited for: 8 -> 1; matrix products, arithmetic and copies ran while one was open for 1% -> 0% of each run, Pallas kernels for 0% -> 0%
where the time goes in v1:
time: 299 us; the launch traced here: 298 us
  waiting for transfers between devices  199 us (67%)
  Pallas kernels  48.5 us (16%)
  blocking collectives  26.9 us (9%)
  between operations  14.8 us (5%)
  matrix products  7.72 us (3%)
    psum x1, waiting for transfers between devices, shards(): w = lax.psum(partial_w, 'past')  199 us
    pallas_call x1, Pallas kernels, iterate(): pl.pallas_call(iterate_kernel, out_shape=(shape, shape), scratch_shapes=[...  48.5 us
    all_gather x1, blocking collectives, shards(): diag_left = lax.all_gather(diag_left[0], 'rows', axis=0, tiled=True)  13.9 us
    all_gather x1, blocking collectives, shards(): diag_right = lax.all_gather(diag_right[0], 'rows', axis=0, tiled=True)  13 us
  transfers between devices with their start and end apart: 1, of which 1 were waited for; matrix products, arithmetic and copies ran while one was open for 0% of the time, Pallas kernels for 0%

profile of v1, /device:TPU:8, one launch (start us, length us, event | category | flops | bytes accessed | tf_op | source)
XLA Modules:
  0.0 298.3 jit_solution(16935287449133805326)
XLA Ops:
  7.2 0.0 copy-start
  7.2 0.0 copy-start.1
  7.2 0.0 all-reduce.2.cloned.1.call-start
  8.0 13.9 %all-gather.1 = f32[1,1024,128]{2,1,0:T(8,128)S(1)} all-gather(f32[1,256,128]{2,1,0:T(8,128)} %param.10), channel_id=3, replica_groups=mesh['rows'=4,'past'=64] {'rows'}, dimensions={1}, use_global_device_ids=true | all-gather | bytes 655360 | tf_op jit(solution)/shard_map/all_gather | solution.py:128
  21.8 13.0 %all-gather = f32[1,1024,128]{2,1,0:T(8,128)S(1)} all-gather(f32[1,256,128]{2,1,0:T(8,128)} %param.11), channel_id=2, replica_groups=mesh['rows'=4,'past'=64] {'rows'}, dimensions={1}, use_global_device_ids=true | all-gather | bytes 655360 | tf_op jit(solution)/shard_map/all_gather | solution.py:129
  34.8 1.1 multiply_bitcast_fusion
  35.9 2.0 convolution_multiply_fusion
  37.9 0.0 copy-done
  38.0 0.6 fusion
  38.5 0.0 copy-done.1
  38.5 5.1 %fusion.1 = f32[1024,1024]{1,0:T(8,128)} fusion(f32[1024,128]{1,0:T(8,128)S(1)} %multiply_bitcast_fusion, f32[1024,128]{1,0:T(8,128)S(1)} %fusion, f32[1024,128]{1,0:T(8,128)S(1)} %bitcast.21, f32[1024,128]{1,0:T(8,128)S(1)} %bitcast.20), kind=kOutput, calls=%fused_computation.3 | convolution fusion | flops 3221749760 | bytes 6291456 | tf_op jit(solution)/shard_map/bk,ck->bc/dot_general | solution.py:136
  43.6 0.0 all-reduce.2.cloned.1.call-update
  43.7 199.3 %all-reduce.2.cloned.1.call-done.w_ref = f32[1024,1024]{1,0:T(8,128)} async-done(((f32[1024,1024]{1,0:T(8,128)}), f32[1024,1024]{1,0:T(8,128)}) %all-reduce.2.cloned.1.call-update) | async-done | bytes 4194320 | tf_op jit(solution)/shard_map/psum | solution.py:137
  242.9 48.5 %iterate.1 = (f32[1024,128]{1,0:T(8,128)}, f32[1024,128]{1,0:T(8,128)}) custom-call(f32[1024,1024]{1,0:T(8,128)} %all-reduce.2.cloned.1.call-done.w_ref, f32[1024,128]{1,0:T(8,128)} %bitcast.22), custom_call_target="tpu_custom_call" | custom-call | tf_op jit(solution)/shard_map/iterate/pallas_call | solution.py:113
Async XLA Ops:
  7.2 30.8 %copy-start = (f32[1,1,1024,128]{3,2,1,0:T(8,128)S(1)}, f32[1,1,1024,128]{3,2,1,0:T(8,128)}, u32[]{:S(2)}) copy-start(f32[1,1,1024,128]{3,2,1,0:T(8,128)} %param.8) | copy-start | bytes 1572868
  7.2 31.4 %copy-start.1 = (f32[1,1024,128]{2,1,0:T(8,128)S(1)}, f32[1,1024,128]{2,1,0:T(8,128)}, u32[]{:S(2)}) copy-start(f32[1,1024,128]{2,1,0:T(8,128)} %param.14) | copy-start | bytes 1572868
  7.2 235.8 %all-reduce.2.cloned.1.call-start = ((), (), s32[]{:S(2)}) async-start(), calls=%async_computation | async-start | bytes 8388608 | tf_op jit(solution)/shard_map/psum | solution.py:137
Sparse Core Ops, SparseCore 0:
  43.8 199.1 all-reduce.1
